TPU v7x, 32 devices: a whole 2x2x4 slice. The times are simulated.
32 devices in a mesh: grp: 2 (over y), node: 4 (over z), sub: 2 (over x), rep: 2 (over core).
Axes of the slice: x: 2, y: 2, z: 4, core: 2. Of those that a mesh axis runs over, the one named last changes fastest.
Arguments:
- meson_nodes: float32 [2, 16, 512, 512], P(None, ('grp', 'node'), 'sub', 'rep'), parts along dimension 1, may hold values from -0.66 to 0.66
- term_nodes: int32 [8, 2], P('grp'), parts along dimension 0, may hold values from 0 to 7, as said below
- weight_codes: int32 [8], P('grp'), parts along dimension 0, may hold values from 0 to 7
- resident_pick: int32 [16], P('grp'), parts along dimension 0, may hold values from 0 to 1
Outputs:
- contracted: float32 [2, 16, 512, 512], P(None, ('grp', 'node'), 'sub', 'rep'), parts along dimension 1
There are 2 independent parts, one for each index of `grp`. A program takes and returns all parts, laid end to end along the dimension named above; each array names one. Nothing has to cross between parts.
Inputs may be any that keep to these rules, and one draw needn't show every extreme that they name: `term_nodes`: node n belongs to owner n // 2. In every term the two nodes differ. The first nodes of at most 2 terms belong to any one owner, and those of exactly 2 terms to some owner.
All inputs are finite; a program needn't handle non-finite values.
Results may differ from a plain program's by a relative error of at most 0.000098.
Values sent between devices are 32-bit elements; how exact they have to be, the bound alone decides.
A program may use at most 64 MiB of HBM per device.

v0:
```python
import jax
import jax.numpy as jnp
from jax import lax
from jax.sharding import PartitionSpec as P


def complex_step(full_left, segment):
    highest = lax.Precision.HIGHEST
    real_part = jnp.einsum(
        "kij,kjl->kil",
        full_left[0],
        segment[0],
        precision=highest,
        preferred_element_type=jnp.float32,
    ) - jnp.einsum(
        "kij,kjl->kil",
        full_left[1],
        segment[1],
        precision=highest,
        preferred_element_type=jnp.float32,
    )
    imag_part = jnp.einsum(
        "kij,kjl->kil",
        full_left[0],
        segment[1],
        precision=highest,
        preferred_element_type=jnp.float32,
    ) + jnp.einsum(
        "kij,kjl->kil",
        full_left[1],
        segment[0],
        precision=highest,
        preferred_element_type=jnp.float32,
    )
    return jnp.stack([real_part, imag_part])


def body(meson_nodes, term_nodes, weight_codes, resident_pick):
    node_count = lax.axis_size("node")
    owned = meson_nodes.shape[1]
    row_count = meson_nodes.shape[2]
    col_count = meson_nodes.shape[3]
    band = row_count // node_count
    total_nodes = owned * node_count
    term_count = term_nodes.shape[0]
    banded = meson_nodes.reshape(2, owned, node_count, band * col_count)
    spread = lax.all_to_all(banded, "node", split_axis=2, concat_axis=1, tiled=True).reshape(
        2, total_nodes, band * col_count
    )
    leading = term_nodes[:, 0]
    trailing = term_nodes[:, 1]
    worker_ids = jnp.arange(node_count, dtype=jnp.int32)
    slot_count = term_count // node_count
    table = jnp.arange(slot_count, dtype=jnp.int32)[None, :] * node_count + worker_ids[:, None]
    active = jnp.ones(table.shape, jnp.float32)
    first_table = leading[table]
    second_table = trailing[table]
    factors = active * (weight_codes[table].astype(jnp.float32) - 3.5) * 0.5
    wanted = jnp.stack([first_table.T, second_table.T], axis=1)
    picked = jnp.take(spread, wanted, axis=1)
    fetched = lax.all_to_all(picked, "node", split_axis=3, concat_axis=3, tiled=True).reshape(
        2, slot_count, 2, row_count, col_count
    )
    left_rows = fetched[:, :, 0]
    right_band = fetched[:, :, 1]
    left_full = lax.all_gather(left_rows, "rep", axis=3, tiled=True)
    products = complex_step(left_full, lax.all_gather(right_band, "sub", axis=2, tiled=True))
    outgoing = products.reshape(2, slot_count, node_count, band * col_count)
    returned = lax.all_to_all(outgoing, "node", split_axis=2, concat_axis=1, tiled=True).reshape(
        2, node_count * slot_count, band * col_count
    )
    node_ids = jnp.arange(total_nodes, dtype=jnp.int32)
    incidence = (first_table.reshape(-1)[:, None] == node_ids[None, :]).astype(jnp.float32) + (
        second_table.reshape(-1)[:, None] == node_ids[None, :]
    ).astype(jnp.float32)
    mixing = factors.reshape(-1)[:, None] * incidence
    summed = jnp.einsum("mn,cmx->cnx", mixing, returned, precision=lax.Precision.HIGHEST)
    owner_sum = lax.all_to_all(
        summed.reshape(2, total_nodes, 1, band * col_count),
        "node",
        split_axis=1,
        concat_axis=2,
        tiled=True,
    ).reshape(2, owned, row_count, col_count)
    sum_full = lax.all_gather(owner_sum, "rep", axis=3, tiled=True)
    own_index = lax.axis_index("node")
    picks = lax.dynamic_slice_in_dim(resident_pick, own_index * owned, owned)
    resident = jnp.take(meson_nodes, picks, axis=1)
    return complex_step(sum_full, lax.all_gather(resident, "sub", axis=2, tiled=True))


def solution(mesh):
    in_specs = (P(None, ("grp", "node"), "sub", "rep"), P("grp", None), P("grp"), P("grp"))
    out_specs = P(None, ("grp", "node"), "sub", "rep")
    return jax.shard_map(body, mesh=mesh, in_specs=in_specs, out_specs=out_specs, check_vma=False)
```

profile of v0, /device:TPU:1, one launch (start us, length us, event | category | flops | bytes accessed | tf_op | source)
XLA Modules:
  0.0 191.4 jit_solution(10941233466209382767)
XLA Ops:
  6.5 1.8 reshape.311
  8.3 1.8 copy.20
  10.1 5.4 %all-to-all-start = ((f32[2,2,4,16384]{3,0,1,2:T(2,128)}), f32[2,2,4,16384]{3,0,1,2:T(2,128)S(1)}, u32[]{:S(2)}, u32[]{:S(2)}) async-start(f32[2,2,4,16384]{3,0,1,2:T(2,128)} %copy.20), calls=%async_computation | async-start | bytes 2097152 | tf_op jit(solution)/shard_map/all_to_all | solution.py:47
  17.1 23.7 %all-to-all-done = f32[2,2,4,16384]{3,0,1,2:T(2,128)S(1)} async-done(((f32[2,2,4,16384]{3,0,1,2:T(2,128)}), f32[2,2,4,16384]{3,0,1,2:T(2,128)S(1)}, u32[]{:S(2)}, u32[]{:S(2)}) %all-to-all-start) | async-done | bytes 1048608 | tf_op jit(solution)/shard_map/all_to_all | solution.py:47
  40.8 1.7 gather_fusion.2
  42.5 1.1 bitcast_select_fusion
  43.6 27.2 %all_to_all.44 = f32[2,1,2,4,16384]{4,2,0,1,3:T(2,128)S(1)} all-to-all(f32[2,1,2,4,16384]{4,2,0,1,3:T(2,128)S(1)} %bitcast_select_fusion), channel_id=1, replica_groups=mesh['grp'=2,'node'=4,'sub'=2,'rep'=2] {'node'}, dimensions={3} | all-to-all | bytes 2097152 | tf_op jit(solution)/shard_map/all_to_all | solution.py:61
  70.7 0.7 copy.22
  71.4 0.7 reshape.313
  72.2 1.0 fusion.18
  73.3 0.7 all-gather.11.cloned.1.call-update
  74.0 20.9 %all-gather.13.cloned.1.call-done = f32[2,1,1,512,256]{4,3,2,0,1:T(8,128)} async-done(((f32[2,1,1,256,256]{4,3,2,0,1:T(8,128)}), f32[2,1,1,512,256]{4,3,2,0,1:T(8,128)}) %all-gather.13.cloned.1.call-update) | async-done | bytes 1048592 | tf_op jit(solution)/shard_map/all_gather | solution.py:67
  94.9 11.2 %all-gather.11.cloned.1.call-done = f32[2,1,1,256,512]{4,3,2,0,1:T(8,128)} async-done(((f32[2,1,1,256,256]{4,3,2,0,1:T(8,128)}), f32[2,1,1,256,512]{4,3,2,0,1:T(8,128)}) %all-gather.11.cloned.1.call-update) | async-done | bytes 1048592 | tf_op jit(solution)/shard_map/all_gather | solution.py:66
  106.0 1.9 fusion.7
  107.9 1.8 convolution_add_fusion.1
  110.6 1.3 convolution_subtract_fusion.1
  111.9 1.2 stack.43
  113.2 1.3 pad_maximum_fusion.1
  114.4 4.7 %all-to-all-start.2 = ((f32[2,1,4,16384]{3,0,1,2:T(2,128)}), f32[2,1,4,16384]{3,0,1,2:T(2,128)S(1)}, u32[]{:S(2)}, u32[]{:S(2)}) async-start(f32[2,1,4,16384]{3,0,1,2:T(2,128)} %pad_maximum_fusion.1), calls=%async_computation.2 | async-start | bytes 1048576 | tf_op jit(solution)/shard_map/all_to_all | solution.py:69
  119.8 1.2 fusion.2
  121.9 11.3 %all-to-all-done.2 = f32[2,1,4,16384]{3,0,1,2:T(2,128)S(1)} async-done(((f32[2,1,4,16384]{3,0,1,2:T(2,128)}), f32[2,1,4,16384]{3,0,1,2:T(2,128)S(1)}, u32[]{:S(2)}, u32[]{:S(2)}) %all-to-all-start.2) | async-done | bytes 524320 | tf_op jit(solution)/shard_map/all_to_all | solution.py:69
  133.2 1.4 convolution_bitcast_fusion
  134.6 0.8 copy.26
  135.4 27.2 %all_to_all.45 = f32[2,8,1,16384]{3,0,2,1:T(2,128)S(1)} all-to-all(f32[2,8,1,16384]{3,0,2,1:T(2,128)S(1)} %copy.26), channel_id=1, replica_groups=mesh['grp'=2,'node'=4,'sub'=2,'rep'=2] {'node'}, dimensions={1} | all-to-all | bytes 2097152 | tf_op jit(solution)/shard_map/all_to_all | solution.py:78
  162.5 0.7 copy.38
  163.2 1.7 reshape.320
  165.0 11.4 %all-gather.7.cloned.1.call-done = f32[2,2,256,512]{3,2,1,0:T(8,128)} async-done(((f32[2,2,256,256]{3,2,1,0:T(8,128)}), f32[2,2,256,512]{3,2,1,0:T(8,128)}) %all-gather.7.cloned.1.call-update) | async-done | bytes 2097168 | tf_op jit(solution)/shard_map/all_gather | solution.py:85
  176.4 2.8 %fusion.3 = f32[2,256,256]{2,1,0:T(8,128)S(1)} fusion(f32[2,2,256,512]{3,2,1,0:T(8,128)} %all-gather.7.cloned.1.call-done, f32[2,2,512,256]{3,2,1,0:T(8,128)} %all-gather.9.cloned.1.call-done), kind=kOutput, calls=%fused_computation.21 | convolution fusion | flops 805306368 | bytes 2621440 | tf_op jit(solution)/shard_map/kij,kjl->kil/dot_general | solution.py:22
  179.2 2.4 %fusion.4 = f32[2,256,256]{2,1,0:T(8,128)S(1)} fusion(f32[2,2,256,512]{3,2,1,0:T(8,128)} %all-gather.7.cloned.1.call-done, f32[2,2,512,256]{3,2,1,0:T(8,128)S(1)} %copy-done.1), kind=kOutput, calls=%fused_computation.22 | convolution fusion | flops 805306368 | bytes 2621440 | tf_op jit(solution)/shard_map/kij,kjl->kil/dot_general | solution.py:9
  181.6 1.1 fusion
  182.7 1.1 fusion.1
  183.9 1.0 pad_maximum_fusion
  (41 shorter events, 4.1 us)
Async XLA Ops:
  6.5 114.7 %copy-start = (s32[4]{0:T(128)S(1)}, s32[4]{0:T(128)}, u32[]{:S(2)}) copy-start(s32[4]{0:T(128)} %param.6) | copy-start | bytes 52
  8.3 7.2 %copy-start.6 = (s32[4,2]{0,1:T(2,128)S(1)}, s32[4,2]{0,1:T(2,128)}, u32[]{:S(2)}) copy-start(s32[4,2]{0,1:T(2,128)} %param.5) | copy-start | bytes 100
  10.1 30.7 %all-to-all-start = ((f32[2,2,4,16384]{3,0,1,2:T(2,128)}), f32[2,2,4,16384]{3,0,1,2:T(2,128)S(1)}, u32[]{:S(2)}, u32[]{:S(2)}) async-start(f32[2,2,4,16384]{3,0,1,2:T(2,128)} %copy.20), calls=%async_computation | async-start | bytes 2097152 | tf_op jit(solution)/shard_map/all_to_all | solution.py:47
  15.5 79.4 %all-gather.13.cloned.1.call-start = ((), (), s32[]{:S(2)}) async-start(), calls=%async_computation.7 | async-start | bytes 1572864 | tf_op jit(solution)/shard_map/all_gather | solution.py:67
  73.2 32.8 %all-gather.11.cloned.1.call-start = ((), (), s32[]{:S(2)}) async-start(), calls=%async_computation.6 | async-start | bytes 1572864 | tf_op jit(solution)/shard_map/all_gather | solution.py:66
  94.9 15.1 %copy-start.3 = (f32[2,1,1,512,256]{4,3,2,0,1:T(8,128)S(1)}, f32[2,1,1,512,256]{4,3,2,0,1:T(8,128)}, u32[]{:S(2)}) copy-start(f32[2,1,1,512,256]{4,3,2,0,1:T(8,128)} %all-gather.13.cloned.1.call-done) | copy-start | bytes 3145732
  106.0 4.0 %copy-start.4 = (f32[2,1,1,256,512]{4,3,2,0,1:T(8,128)S(1)}, f32[2,1,1,256,512]{4,3,2,0,1:T(8,128)}, u32[]{:S(2)}) copy-start(f32[2,1,1,256,512]{4,3,2,0,1:T(8,128)} %all-gather.11.cloned.1.call-done) | copy-start | bytes 3145732
  110.6 8.5 %copy-start.7 = (s32[8]{0:T(128)S(1)}, s32[8]{0:T(128)}, u32[]{:S(2)}) copy-start(s32[8]{0:T(128)} %param.7) | copy-start | bytes 100
  110.6 8.6 %copy-start.5 = (f32[2,2,256,256]{3,2,1,0:T(8,128)S(1)}, f32[2,2,256,256]{3,2,1,0:T(8,128)}, u32[]{:S(2)}) copy-start(f32[2,2,256,256]{3,2,1,0:T(8,128)} %param.4) | copy-start | bytes 3145732
  114.4 18.8 %all-to-all-start.2 = ((f32[2,1,4,16384]{3,0,1,2:T(2,128)}), f32[2,1,4,16384]{3,0,1,2:T(2,128)S(1)}, u32[]{:S(2)}, u32[]{:S(2)}) async-start(f32[2,1,4,16384]{3,0,1,2:T(2,128)} %pad_maximum_fusion.1), calls=%async_computation.2 | async-start | bytes 1048576 | tf_op jit(solution)/shard_map/all_to_all | solution.py:69
  119.1 45.9 %all-gather.9.cloned.1.call-start = ((), (), s32[]{:S(2)}) async-start(), calls=%async_computation.5 | async-start | bytes 3145728 | tf_op jit(solution)/shard_map/all_gather | solution.py:89
  121.0 55.4 %all-gather.7.cloned.1.call-start = ((), (), s32[]{:S(2)}) async-start(), calls=%async_computation.4 | async-start | bytes 3145728 | tf_op jit(solution)/shard_map/all_gather | solution.py:85
  165.0 14.2 %copy-start.1 = (f32[2,2,512,256]{3,2,1,0:T(8,128)S(1)}, f32[2,2,512,256]{3,2,1,0:T(8,128)}, u32[]{:S(2)}) copy-start(f32[2,2,512,256]{3,2,1,0:T(8,128)} %all-gather.9.cloned.1.call-done) | copy-start | bytes 6291460
  176.4 5.2 %copy-start.2 = (f32[2,2,256,512]{3,2,1,0:T(8,128)S(1)}, f32[2,2,256,512]{3,2,1,0:T(8,128)}, u32[]{:S(2)}) copy-start(f32[2,2,256,512]{3,2,1,0:T(8,128)} %all-gather.7.cloned.1.call-done) | copy-start | bytes 6291460
Sparse Core Ops, SparseCore 0:
  73.3 21.4 all-gather.12
  96.4 9.5 all-gather.10
  121.4 34.1 all-gather.8
  165.1 11.2 all-gather.6
where the time goes:
time: 192 us; the launch traced here: 191 us
  waiting for transfers between devices  79.2 us (41%)
  blocking collectives  54.3 us (28%)
  local copies, waits for them, and re-layouts  15.1 us (8%)
  matrix products  14.4 us (8%)
  between operations  13.4 us (7%)
  starting transfers between devices  10.3 us (5%)
  other arithmetic  4.75 us (2%)
    all_to_all x1, blocking collectives, body(): lax.all_to_all(picked, 'node', split_axis=3, concat_axis=3, tiled=True)  27.2 us
    all_to_all x1, blocking collectives, body(): lax.all_to_all(summed.reshape(2, total_nodes, 1, band * col_count), 'node...  27.2 us
    all_to_all x1, waiting for transfers between devices, body(): lax.all_to_all(banded, 'node', split_axis=2, concat_axis=1, tiled=True)  23.7 us
    all_gather x1, waiting for transfers between devices, body(): lax.all_gather(right_band, 'sub', axis=2, tiled=True)  20.9 us
    all_gather x1, waiting for transfers between devices, body(): sum_full = lax.all_gather(owner_sum, 'rep', axis=3, tiled=True)  11.4 us
    all_to_all x1, waiting for transfers between devices, body(): lax.all_to_all(outgoing, 'node', split_axis=2, concat_axis=1, tiled=True)  11.3 us
    all_gather x1, waiting for transfers between devices, body(): left_full = lax.all_gather(left_rows, 'rep', axis=3, tiled=True)  11.2 us
    all_to_all x1, starting transfers between devices, body(): lax.all_to_all(banded, 'node', split_axis=2, concat_axis=1, tiled=True)  5.41 us
  transfers between devices with their start and end apart: 6, of which 5 were waited for; matrix products, arithmetic and copies ran while one was open for 5% of the time, Pallas kernels for 0%

commit v1 on v0

--- a/solution.py
+++ b/solution.py
@@ -1,6 +1,10 @@
+import functools
+
 import jax
 import jax.numpy as jnp
 from jax import lax
+from jax.experimental import pallas as pl
+from jax.experimental.pallas import tpu as pltpu
 from jax.sharding import PartitionSpec as P
 
 
@@ -35,7 +39,7 @@
     return jnp.stack([real_part, imag_part])
 
 
-def body(meson_nodes, term_nodes, weight_codes, resident_pick):
+def wide_body(meson_nodes, term_nodes, weight_codes, resident_pick):
     node_count = lax.axis_size("node")
     owned = meson_nodes.shape[1]
     row_count = meson_nodes.shape[2]
@@ -89,6 +93,282 @@
     return complex_step(sum_full, lax.all_gather(resident, "sub", axis=2, tiled=True))
 
 
+MESH = pl.DeviceIdType.MESH
+FOREIGN = 2
+
+
+def split(value):
+    high = value.astype(jnp.bfloat16)
+    return high, (value - high.astype(jnp.float32)).astype(jnp.bfloat16)
+
+
+def mul(left, right):
+    def dot(p, q):
+        return jnp.dot(p, q, preferred_element_type=jnp.float32)
+
+    return dot(left[0], right[0]) + (dot(left[0], right[1]) + dot(left[1], right[0]))
+
+
+def complex_mul(lefts, rights):
+    real = imag = None
+    for (a0, a1), (b0, b1) in zip(lefts, rights):
+        a0, a1, b0, b1 = split(a0), split(a1), split(b0), split(b1)
+        re = mul(a0, b0) - mul(a1, b1)
+        im = mul(a0, b1) + mul(a1, b0)
+        real = re if real is None else real + re
+        imag = im if imag is None else imag + im
+    return real, imag
+
+
+def line_kernel(
+    length, owned, terms,
+    x_ref, tn_ref, wc_ref, rp_ref, out_ref,
+    nodes, rows, sums,
+    loc_sem, z_send, z_recv, c_send, c_recv, x_send, x_recv, s_send, s_recv,
+):
+    z = lax.axis_index("node")
+    x = lax.axis_index("sub")
+    c = lax.axis_index("rep")
+    g = lax.axis_index("grp")
+    left = (g, z - 1, x, c)
+    right = (g, z + 1, x, c)
+    across = (g, z, 1 - x, c)
+    twin = (g, z, x, 1 - c)
+    has_left = z > 0
+    has_right = z < length - 1
+    pieces = [(j, m) for j in range(owned) for m in range(2)]
+
+    def remote(src, dst, send, recv, device):
+        return pltpu.make_async_remote_copy(
+            src_ref=src, dst_ref=dst, send_sem=send, recv_sem=recv, device_id=device, device_id_type=MESH
+        )
+
+    barrier = pltpu.get_barrier_semaphore()
+    for device in (across, twin):
+        pl.semaphore_signal(barrier, inc=1, device_id=device, device_id_type=MESH)
+
+    @pl.when(has_left)
+    def _():
+        pl.semaphore_signal(barrier, inc=1, device_id=left, device_id_type=MESH)
+
+    @pl.when(has_right)
+    def _():
+        pl.semaphore_signal(barrier, inc=1, device_id=right, device_id_type=MESH)
+
+    pl.semaphore_wait(barrier, 2 + has_left.astype(jnp.int32) + has_right.astype(jnp.int32))
+
+    def node_at(owner, j, m):
+        return nodes.at[c, owner * owned + j, m]
+
+    def z_copy(way, step, j, m):
+        owner = z + step if way == 0 else z - step
+        src = x_ref.at[m, j] if step == 0 else node_at(owner, j, m)
+        return remote(
+            src, node_at(owner, j, m), z_send.at[way, step, j, m], z_recv.at[way, step, j, m],
+            left if way == 0 else right,
+        )
+
+    def z_sends(way, step):
+        if way == 0:
+            return jnp.logical_and(has_left, z + step <= length - 1)
+        return jnp.logical_and(has_right, z - step >= 0)
+
+    def z_arrival(way, step, j, m):
+        owner = z + 1 + step if way == 0 else z - 1 - step
+        return remote(
+            node_at(owner, j, m), node_at(owner, j, m), z_send.at[way, step, j, m], z_recv.at[way, step, j, m],
+            left if way == 0 else right,
+        )
+
+    def c_copy(owner, j, m, own=False):
+        src = x_ref.at[m, j] if own else node_at(owner, j, m)
+        return remote(src, node_at(owner, j, m), c_send.at[owner, j, m], c_recv.at[owner, j, m], twin)
+
+    def x_own(j, m):
+        return remote(x_ref.at[m, j], rows.at[x, j, m], x_send.at[j, m], x_recv.at[j, m], across)
+
+    def x_slot(s, m):
+        k = owned + s
+        return remote(rows.at[x, k, m], rows.at[x, k, m], x_send.at[k, m], x_recv.at[k, m], across)
+
+    for j, m in pieces:
+        for way in range(2):
+
+            @pl.when(z_sends(way, 0))
+            def _():
+                z_copy(way, 0, j, m).start()
+
+        x_own(j, m).start()
+    local = []
+    for j, m in pieces:
+        for i, dst in enumerate((node_at(z, j, m), rows.at[x, j, m])):
+            copy = pltpu.make_async_copy(x_ref.at[m, j], dst, loc_sem.at[i, j, m])
+            copy.start()
+            local.append(copy)
+        c_copy(z, j, m, own=True).start()
+    for copy in local:
+        copy.wait()
+
+    far = jnp.where(z < length // 2, length - 1, 0)
+    late = far * owned + owned - 1
+    firsts = [tn_ref[t, 0] for t in range(terms)]
+    seconds = [tn_ref[t, 1] for t in range(terms)]
+    home = z * owned
+
+    def mine(n):
+        return jnp.logical_and(n >= home, n < home + owned)
+
+    needs = [jnp.logical_and(mine(a), jnp.logical_not(mine(b))) for a, b in zip(firsts, seconds)]
+    slot1 = home
+    for need, b in zip(needs, seconds):
+        slot1 = jnp.where(jnp.logical_and(need, slot1 != late), b, slot1)
+    slot0 = home
+    for need, b in zip(needs, seconds):
+        slot0 = jnp.where(jnp.logical_and(need, b != slot1), b, slot0)
+
+    def stage(s, m):
+        wanted = slot1 if s else slot0
+        chosen = nodes[c, home, m]
+        for k in range(length):
+            owner = lax.rem(far + 1 + k, length)
+            for j in range(owned):
+                if s == 0 and k == length - 1 and j == owned - 1:
+                    continue
+                n = owner * owned + j
+                chosen = jnp.where(wanted == n, nodes[c, n, m], chosen)
+        rows[x, owned + s, m] = chosen
+        x_slot(s, m).start()
+
+    for step in range(length - 1):
+        for j, m in pieces:
+            for way in range(2):
+                owner = z + 1 + step if way == 0 else z - 1 - step
+                arrives = owner <= length - 1 if way == 0 else owner >= 0
+
+                @pl.when(arrives)
+                def _():
+                    z_arrival(way, step, j, m).wait_recv()
+                    c_copy(owner, j, m).start()
+
+                if step < length - 2:
+
+                    @pl.when(jnp.logical_and(arrives, z_sends(way, step + 1)))
+                    def _():
+                        z_copy(way, step + 1, j, m).start()
+
+            if step == length - 2:
+                stage(j, m)
+
+    for owner in range(length):
+        for j, m in pieces:
+            remote(
+                nodes.at[1 - c, owner * owned + j, m], nodes.at[1 - c, owner * owned + j, m],
+                c_send.at[owner, j, m], c_recv.at[owner, j, m], twin,
+            ).wait_recv()
+    for k in range(owned + FOREIGN):
+        for m in range(2):
+            remote(
+                rows.at[1 - x, k, m], rows.at[1 - x, k, m], x_send.at[k, m], x_recv.at[k, m], across
+            ).wait_recv()
+
+    for t in range(terms):
+        a, b = firsts[t], seconds[t]
+        k = jnp.where(mine(b), b - home, jnp.where(b == slot1, owned + 1, owned))
+        real, imag = complex_mul(
+            [(nodes[h, a, 0], nodes[h, a, 1]) for h in range(2)],
+            [(rows[h, k, 0], rows[h, k, 1]) for h in range(2)],
+        )
+        factor = (wc_ref[t].astype(jnp.float32) - 3.5) * 0.5
+        for j in range(owned):
+            n = home + j
+            count = (a == n).astype(jnp.float32) + (b == n).astype(jnp.float32)
+            weight = factor * count
+            for m, part in ((0, real), (1, imag)):
+                if t == 0:
+                    sums[c, j, m] = weight * part
+                else:
+                    sums[c, j, m] = sums[c, j, m] + weight * part
+
+    def s_copy(h, j, m):
+        return remote(sums.at[h, j, m], sums.at[h, j, m], s_send.at[j, m], s_recv.at[j, m], twin)
+
+    for j, m in pieces:
+        s_copy(c, j, m).start()
+    for j, m in pieces:
+        s_copy(1 - c, j, m).wait_recv()
+    for j in range(owned):
+        pick = rp_ref[home + j]
+        real, imag = complex_mul(
+            [(sums[h, j, 0], sums[h, j, 1]) for h in range(2)],
+            [(rows[h, pick, 0], rows[h, pick, 1]) for h in range(2)],
+        )
+        out_ref[0, j] = real
+        out_ref[1, j] = imag
+
+    for j, m in pieces:
+        s_copy(c, j, m).wait_send()
+        x_own(j, m).wait_send()
+    for s in range(FOREIGN):
+        for m in range(2):
+            x_slot(s, m).wait_send()
+    for step in range(length - 1):
+        for j, m in pieces:
+            for way in range(2):
+
+                @pl.when(z_sends(way, step))
+                def _():
+                    z_copy(way, step, j, m).wait_send()
+
+    for owner in range(length):
+        for j, m in pieces:
+            c_copy(owner, j, m).wait_send()
+
+
+def line_body(meson_nodes, term_nodes, weight_codes, resident_pick):
+    length = lax.axis_size("node")
+    _, owned, height, width = meson_nodes.shape
+    terms = term_nodes.shape[0]
+    block = (height, width)
+    vmem = pl.BlockSpec(memory_space=pltpu.VMEM)
+    smem = pl.BlockSpec(memory_space=pltpu.SMEM)
+    dma = pltpu.SemaphoreType.DMA
+    slots = owned + FOREIGN
+    return pl.pallas_call(
+        functools.partial(line_kernel, length, owned, terms),
+        out_shape=jax.ShapeDtypeStruct(meson_nodes.shape, jnp.float32),
+        in_specs=[pl.BlockSpec(memory_space=pl.ANY), smem, smem, smem],
+        out_specs=vmem,
+        scratch_shapes=[
+            pltpu.VMEM((2, length * owned, 2) + block, jnp.float32),
+            pltpu.VMEM((2, slots, 2) + block, jnp.float32),
+            pltpu.VMEM((2, owned, 2) + block, jnp.float32),
+            dma((2, owned, 2)),
+            dma((2, length - 1, owned, 2)),
+            dma((2, length - 1, owned, 2)),
+            dma((length, owned, 2)),
+            dma((length, owned, 2)),
+            dma((slots, 2)),
+            dma((slots, 2)),
+            dma((owned, 2)),
+            dma((owned, 2)),
+        ],
+        compiler_params=pltpu.CompilerParams(
+            collective_id=0, has_side_effects=True, vmem_limit_bytes=56 << 20
+        ),
+    )(meson_nodes, term_nodes, weight_codes, resident_pick)
+
+
+def body(meson_nodes, term_nodes, weight_codes, resident_pick):
+    length, owned = lax.axis_size("node"), meson_nodes.shape[1]
+    square = meson_nodes.shape[2] == meson_nodes.shape[3]
+    halves = lax.axis_size("sub") == 2 and lax.axis_size("rep") == 2
+    held = 2 * length * meson_nodes.size * 4
+    fits = held <= 16 << 20 and term_nodes.shape[0] <= 8
+    if square and halves and fits and owned == FOREIGN and length > 2:
+        return line_body(meson_nodes, term_nodes, weight_codes, resident_pick)
+    return wide_body(meson_nodes, term_nodes, weight_codes, resident_pick)
+
+
 def solution(mesh):
     in_specs = (P(None, ("grp", "node"), "sub", "rep"), P("grp", None), P("grp"), P("grp"))
     out_specs = P(None, ("grp", "node"), "sub", "rep")

time: 192 us -> 93.9 us (0.49)
  Pallas kernels: 0 us -> 90.1 us
  waiting for transfers between devices: 79.2 us -> 0 us
  blocking collectives: 54.3 us -> 0 us
  matrix products: 14.4 us -> 0 us
  between operations: 13.4 us -> 0.01 us
  local copies, waits for them, and re-layouts: 15.1 us -> 3.62 us
  starting transfers between devices: 10.3 us -> 0 us
  other arithmetic: 4.75 us -> 0 us
    pallas_call x0 -> x1, Pallas kernels: none -> 90.1 us  [line_body(): pl.pallas_call(functools.partial(line_kernel, length, owned, terms), out_...]
    all_to_all x2 -> x0, blocking collectives: 54.3 us -> none  [the longest x1 27.2 us: body(): lax.all_to_all(picked, 'node', split_axis=3, concat_axis=3, tiled=True)]
    all_gather x4 -> x0, waiting for transfers between devices: 43.4 us -> none  [the longest x1 20.9 us: body(): lax.all_gather(right_band, 'sub', axis=2, tiled=True)]
    all_to_all x2 -> x0, waiting for transfers between devices: 35 us -> none  [the longest x1 23.7 us: body(): lax.all_to_all(banded, 'node', split_axis=2, concat_axis=1, tiled=True)]
    dot_general x9 -> x0, matrix products: 14.4 us -> none  [the longest x2 4.7 us: complex_step(): jnp.einsum('kij,kjl->kil', full_left[0], segment[1], precision=highest, p...]
    all_to_all x2 -> x0, starting transfers between devices: 10.1 us -> none  [the longest x1 5.41 us: body(): lax.all_to_all(banded, 'node', split_axis=2, concat_axis=1, tiled=True)]
    reshape x5 -> x0, local copies, waits for them, and re-layouts: 6.76 us -> none  [the longest x2 3.53 us: body(): banded = meson_nodes.reshape(2, owned, node_count, band * col_count)]
    gather x5 -> x0, local copies, waits for them, and re-layouts: 4.2 us -> none  [the longest x1 1.67 us: body(): picked = jnp.take(spread, wanted, axis=1)]
  transfers between devices with their start and end apart: 6 -> 0, of which waited for: 5 -> 0; matrix products, arithmetic and copies ran while one was open for 5% -> 0% of each run, Pallas kernels for 0% -> 0%
where the time goes in v1:
time: 93.9 us; the launch traced here: 93.7 us
  Pallas kernels  90.1 us (96%)
  local copies, waits for them, and re-layouts  3.62 us (4%)
    pallas_call x1, Pallas kernels, line_body(): pl.pallas_call(functools.partial(line_kernel, length, owned, terms), out_...  90.1 us
    unnamed x2, local copies, waits for them, and re-layouts  3.62 us

profile of v1, /device:TPU:1, one launch (start us, length us, event | category | flops | bytes accessed | tf_op | source)
XLA Modules:
  0.0 93.7 jit_solution(5715866744170105516)
XLA Ops:
  0.0 1.3 %copy.5.tn_ref = s32[4,2]{1,0:T(4,128)} copy(s32[4,2]{0,1:T(2,128)} %param.5) | data formatting | bytes 64 | tf_op args[1]
  1.3 90.1 %shard_map.46 = f32[2,2,256,256]{3,2,1,0:T(8,128)} custom-call(f32[2,2,256,256]{3,2,1,0:T(8,128)} %x_ref.1, s32[4,2]{1,0:T(4,128)} %copy.5.tn_ref, s32[4]{0:T(128)} %wc_ref.1, s32[8]{0:T(128)} %rp_ref.1), custom_call_target="tpu_custom_call" | custom-call | tf_op jit(solution)/shard_map/pallas_call | solution.py:336
  91.4 2.3 %copy.7 = f32[2,2,256,256]{3,2,1,0:T(8,128)} copy(f32[2,2,256,256]{3,2,1,0:T(8,128)} %shard_map.46) | data formatting | bytes 2097152

commit v2 on v0

--- a/solution.py
+++ b/solution.py
@@ -1,6 +1,10 @@
+import functools
+
 import jax
 import jax.numpy as jnp
 from jax import lax
+from jax.experimental import pallas as pl
+from jax.experimental.pallas import tpu as pltpu
 from jax.sharding import PartitionSpec as P
 
 
@@ -35,7 +39,7 @@
     return jnp.stack([real_part, imag_part])
 
 
-def body(meson_nodes, term_nodes, weight_codes, resident_pick):
+def wide_body(meson_nodes, term_nodes, weight_codes, resident_pick):
     node_count = lax.axis_size("node")
     owned = meson_nodes.shape[1]
     row_count = meson_nodes.shape[2]
@@ -89,6 +93,367 @@
     return complex_step(sum_full, lax.all_gather(resident, "sub", axis=2, tiled=True))
 
 
+MESH = pl.DeviceIdType.MESH
+PIECES = 2
+FOREIGN = 2
+
+
+def split(value):
+    high = value.astype(jnp.bfloat16)
+    return high, (value - high.astype(jnp.float32)).astype(jnp.bfloat16)
+
+
+def mul(left, right):
+    def dot(p, q):
+        return jnp.dot(p, q, preferred_element_type=jnp.float32)
+
+    return dot(left[0], right[0]) + (dot(left[0], right[1]) + dot(left[1], right[0]))
+
+
+def complex_mul(a0, a1, b0, b1):
+    left, right = split(a0), split(b0)
+    both = mul(left, right)
+    left, right = split(a1), split(b1)
+    other = mul(left, right)
+    cross = mul(split(a0 + a1), split(b0 + b1))
+    return both - other, cross - both - other
+
+
+def line_kernel(
+    length, owned, terms,
+    x_ref, tn_ref, wc_ref, rp_ref, out_ref,
+    nodes, rows, others, sums, picked,
+    loc_sem, z_send, z_recv, c_send, c_recv, x_send, x_recv, s_send, s_recv,
+):
+    z = lax.axis_index("node")
+    x = lax.axis_index("sub")
+    c = lax.axis_index("rep")
+    g = lax.axis_index("grp")
+    left = (g, z - 1, x, c)
+    right = (g, z + 1, x, c)
+    across = (g, z, 1 - x, c)
+    twin = (g, z, x, 1 - c)
+    has_left = z > 0
+    has_right = z < length - 1
+    height = x_ref.shape[2] // PIECES
+    pieces = [(j, m, r) for j in range(owned) for m in range(2) for r in range(PIECES)]
+
+    def band(r):
+        return pl.ds(r * height, height)
+
+    def remote(src, dst, send, recv, device):
+        return pltpu.make_async_remote_copy(
+            src_ref=src, dst_ref=dst, send_sem=send, recv_sem=recv, device_id=device, device_id_type=MESH
+        )
+
+    barrier = pltpu.get_barrier_semaphore()
+    for device in (across, twin):
+        pl.semaphore_signal(barrier, inc=1, device_id=device, device_id_type=MESH)
+
+    @pl.when(has_left)
+    def _():
+        pl.semaphore_signal(barrier, inc=1, device_id=left, device_id_type=MESH)
+
+    @pl.when(has_right)
+    def _():
+        pl.semaphore_signal(barrier, inc=1, device_id=right, device_id_type=MESH)
+
+    pl.semaphore_wait(barrier, 2 + has_left.astype(jnp.int32) + has_right.astype(jnp.int32))
+
+    def node_at(owner, j, m, r):
+        return nodes.at[c, owner * owned + j, m, band(r)]
+
+    def own_at(j, m, r):
+        return x_ref.at[m, j, band(r)]
+
+    def reach(way, step):
+        return z + step if way == 0 else z - step
+
+    def inside(owner):
+        return jnp.logical_and(owner >= 0, owner <= length - 1)
+
+    def to_end(way):
+        return z == (1 if way == 0 else length - 2)
+
+    def z_sends(way, step):
+        found = jnp.logical_and(has_left if way == 0 else has_right, inside(reach(way, step)))
+        return jnp.logical_and(found, jnp.logical_not(to_end(way))) if step == 0 else found
+
+    def z_arrives(way, step):
+        found = inside(reach(way, step + 1))
+        return jnp.logical_and(found, z != (0 if way == 0 else length - 1)) if step == 0 else found
+
+    def z_copy(way, step, j, m, r, src):
+        return remote(
+            src, node_at(reach(way, step), j, m, r), z_send.at[way, step, j, m, r],
+            z_recv.at[way, step, j, m, r], left if way == 0 else right,
+        )
+
+    def c_copy(owner, j, m, r, src):
+        return remote(
+            src, node_at(owner, j, m, r), c_send.at[owner, j, m, r], c_recv.at[owner, j, m, r], twin
+        )
+
+    def x_copy(k, m, r, src):
+        return remote(src, others.at[k, m, band(r)], x_send.at[k, m, r], x_recv.at[k, m, r], across)
+
+    def s_copy(h, j, m):
+        return remote(sums.at[h, j, m], sums.at[h, j, m], s_send.at[j, m], s_recv.at[j, m], twin)
+
+    for way in range(2):
+
+        @pl.when(z_sends(way, 0))
+        def _():
+            for piece in pieces:
+                z_copy(way, 0, *piece, own_at(*piece)).start()
+
+    for piece in pieces:
+        x_copy(*piece, own_at(*piece)).start()
+    local = []
+    for j, m, r in pieces:
+        for i, dst in enumerate((node_at(z, j, m, r), rows.at[j, m, band(r)])):
+            copy = pltpu.make_async_copy(own_at(j, m, r), dst, loc_sem.at[i, j, m, r])
+            copy.start()
+            local.append(copy)
+        c_copy(z, j, m, r, own_at(j, m, r)).start()
+
+    firsts = [tn_ref[t, 0] for t in range(terms)]
+    seconds = [tn_ref[t, 1] for t in range(terms)]
+    spots = (length - 2) * owned
+
+    def holds(owner, n):
+        return jnp.logical_and(n >= owner * owned, n < owner * owned + owned)
+
+    def rank_of(end, n):
+        owner = n // owned
+        return jnp.where(end == 0, owner, length - 1 - owner) * owned + n - owner * owned
+
+    def node_of(end, rank):
+        far = rank // owned
+        return jnp.where(end == 0, far, length - 1 - far) * owned + rank % owned
+
+    def partner_ranks(end):
+        ranks = []
+        for a, b in zip(firsts, seconds):
+            here, there = holds(end, a), holds(end, b)
+            rank = jnp.where(here, rank_of(end, b), rank_of(end, a))
+            ranks.append(jnp.where(here != there, rank, owned))
+        below, found = length * owned, []
+        for _ in range(spots):
+            best = owned
+            for rank in ranks:
+                best = jnp.where(jnp.logical_and(rank < below, rank > best), rank, best)
+            found.append(best)
+            below = best
+        return found[::-1]
+
+    end = jnp.where(z < length // 2, 0, length - 1)
+    wanted_ranks = partner_ranks(end)
+    at_end = z == end
+
+    def entry(n):
+        place = z * owned
+        rank = rank_of(end, n)
+        for i in range(spots):
+            place = jnp.where(wanted_ranks[i] == rank, node_of(end, 2 * owned + i), place)
+        return jnp.where(jnp.logical_and(at_end, jnp.logical_not(holds(z, n))), place, n)
+
+    far = length - 1 - end
+    late = far * owned + owned - 1
+    home = z * owned
+    left_entries = [entry(a) for a in firsts]
+    right_entries = [entry(b) for b in seconds]
+    needs = [
+        jnp.logical_and(holds(z, a), jnp.logical_not(holds(z, b))) for a, b in zip(firsts, seconds)
+    ]
+    slot1 = home
+    for need, e in zip(needs, right_entries):
+        slot1 = jnp.where(jnp.logical_and(need, slot1 != late), e, slot1)
+    slot0 = home
+    for need, e in zip(needs, right_entries):
+        slot0 = jnp.where(jnp.logical_and(need, e != slot1), e, slot0)
+
+    for copy in local:
+        copy.wait()
+
+    def pick(i, m, r):
+        chosen = nodes[c, node_of(end, owned), m, band(r)]
+        for rank in range(owned + 1, 2 * owned + i + 1):
+            chosen = jnp.where(
+                wanted_ranks[i] == rank, nodes[c, node_of(end, rank), m, band(r)], chosen
+            )
+        picked[i, m, band(r)] = chosen
+
+    def stage(s, m, r):
+        wanted = slot1 if s else slot0
+        chosen = nodes[c, home, m, band(r)]
+        for k in range(length):
+            owner = lax.rem(far + 1 + k, length)
+            for j in range(owned):
+                if s == 0 and k == length - 1 and j == owned - 1:
+                    continue
+                n = owner * owned + j
+                chosen = jnp.where(wanted == n, nodes[c, n, m, band(r)], chosen)
+        rows[owned + s, m, band(r)] = chosen
+        x_copy(owned + s, m, r, rows.at[owned + s, m, band(r)]).start()
+
+    depth = jnp.maximum(z, length - 1 - z) - 1
+    for step in range(length - 1):
+        for j, m, r in pieces:
+            for way in range(2):
+
+                @pl.when(z_arrives(way, step))
+                def _():
+                    owner = reach(way, step + 1)
+                    src = node_at(owner, j, m, r)
+                    remote(
+                        src, src, z_send.at[way, step, j, m, r], z_recv.at[way, step, j, m, r],
+                        left if way == 0 else right,
+                    ).wait_recv()
+                    c_copy(owner, j, m, r, src).start()
+
+                if step < length - 2:
+                    goes = jnp.logical_and(z_arrives(way, step), z_sends(way, step + 1))
+
+                    @pl.when(jnp.logical_and(goes, jnp.logical_not(to_end(way))))
+                    def _():
+                        z_copy(way, step + 1, j, m, r, node_at(reach(way, step + 1), j, m, r)).start()
+
+                    @pl.when(jnp.logical_and(goes, to_end(way)))
+                    def _():
+                        i = step * owned + j
+                        pick(i, m, r)
+                        z_copy(way, step + 1, j, m, r, picked.at[i, m, band(r)]).start()
+
+            if step >= length // 2 - 1:
+
+                @pl.when(depth == step)
+                def _():
+                    stage(j, m, r)
+
+    def filled(owner):
+        beside = jnp.where(end == 0, 1, length - 2)
+        return jnp.logical_not(jnp.logical_and(at_end, owner == beside))
+
+    for owner in range(length):
+
+        @pl.when(filled(owner))
+        def _():
+            for j, m, r in pieces:
+                dst = nodes.at[1 - c, owner * owned + j, m, band(r)]
+                remote(dst, dst, c_send.at[owner, j, m, r], c_recv.at[owner, j, m, r], twin).wait_recv()
+
+    def products(h, held, fresh):
+        for t in range(terms):
+            a, b = firsts[t], seconds[t]
+            e, f = left_entries[t], right_entries[t]
+            k = jnp.where(holds(z, b), b - home, jnp.where(f == slot1, owned + 1, owned))
+            parts = complex_mul(nodes[h, e, 0], nodes[h, e, 1], held[k, 0], held[k, 1])
+            factor = (wc_ref[t].astype(jnp.float32) - 3.5) * 0.5
+            for j in range(owned):
+                n = home + j
+                count = (a == n).astype(jnp.float32) + (b == n).astype(jnp.float32)
+                weight = factor * count
+                for m in range(2):
+                    if t == 0 and fresh:
+                        sums[c, j, m] = weight * parts[m]
+                    else:
+                        sums[c, j, m] = sums[c, j, m] + weight * parts[m]
+
+    products(x, rows, True)
+    for k in range(owned + FOREIGN):
+        for m in range(2):
+            for r in range(PIECES):
+                dst = others.at[k, m, band(r)]
+                remote(dst, dst, x_send.at[k, m, r], x_recv.at[k, m, r], across).wait_recv()
+    products(1 - x, others, False)
+
+    for j in range(owned):
+        for m in range(2):
+            s_copy(c, j, m).start()
+    for h in (c, 1 - c):
+        for j in range(owned):
+            if h is not c:
+                for m in range(2):
+                    s_copy(h, j, m).wait_recv()
+            choice = rp_ref[home + j]
+            here = [jnp.where(h == x, rows[choice, m], others[choice, m]) for m in range(2)]
+            parts = complex_mul(sums[h, j, 0], sums[h, j, 1], here[0], here[1])
+            for m in range(2):
+                out_ref[m, j] = parts[m] if h is c else out_ref[m, j] + parts[m]
+
+    for j in range(owned):
+        for m in range(2):
+            s_copy(c, j, m).wait_send()
+    for piece in pieces:
+        x_copy(*piece, own_at(*piece)).wait_send()
+    for s in range(FOREIGN):
+        for m in range(2):
+            for r in range(PIECES):
+                x_copy(owned + s, m, r, rows.at[owned + s, m, band(r)]).wait_send()
+    for step in range(length - 1):
+        for way in range(2):
+
+            @pl.when(z_sends(way, step))
+            def _():
+                for piece in pieces:
+                    z_copy(way, step, *piece, own_at(*piece)).wait_send()
+
+    for owner in range(length):
+
+        @pl.when(filled(owner))
+        def _():
+            for piece in pieces:
+                c_copy(owner, *piece, own_at(*piece)).wait_send()
+
+
+def line_body(meson_nodes, term_nodes, weight_codes, resident_pick):
+    length = lax.axis_size("node")
+    _, owned, height, width = meson_nodes.shape
+    terms = term_nodes.shape[0]
+    block = (height, width)
+    vmem = pl.BlockSpec(memory_space=pltpu.VMEM)
+    smem = pl.BlockSpec(memory_space=pltpu.SMEM)
+    dma = pltpu.SemaphoreType.DMA
+    slots = owned + FOREIGN
+    return pl.pallas_call(
+        functools.partial(line_kernel, length, owned, terms),
+        out_shape=jax.ShapeDtypeStruct(meson_nodes.shape, jnp.float32),
+        in_specs=[pl.BlockSpec(memory_space=pl.ANY), smem, smem, smem],
+        out_specs=vmem,
+        scratch_shapes=[
+            pltpu.VMEM((2, length * owned, 2) + block, jnp.float32),
+            pltpu.VMEM((slots, 2) + block, jnp.float32),
+            pltpu.VMEM((slots, 2) + block, jnp.float32),
+            pltpu.VMEM((2, owned, 2) + block, jnp.float32),
+            pltpu.VMEM(((length - 2) * owned, 2) + block, jnp.float32),
+            dma((2, owned, 2, PIECES)),
+            dma((2, length - 1, owned, 2, PIECES)),
+            dma((2, length - 1, owned, 2, PIECES)),
+            dma((length, owned, 2, PIECES)),
+            dma((length, owned, 2, PIECES)),
+            dma((slots, 2, PIECES)),
+            dma((slots, 2, PIECES)),
+            dma((owned, 2)),
+            dma((owned, 2)),
+        ],
+        compiler_params=pltpu.CompilerParams(
+            collective_id=0, has_side_effects=True, vmem_limit_bytes=56 << 20
+        ),
+    )(meson_nodes, term_nodes, weight_codes, resident_pick)
+
+
+def body(meson_nodes, term_nodes, weight_codes, resident_pick):
+    length, owned = lax.axis_size("node"), meson_nodes.shape[1]
+    square = meson_nodes.shape[2] == meson_nodes.shape[3]
+    halves = lax.axis_size("sub") == 2 and lax.axis_size("rep") == 2
+    held = 2 * length * meson_nodes.size * 4
+    fits = held <= 16 << 20 and term_nodes.shape[0] <= (length - 2) * owned
+    if square and halves and fits and owned == FOREIGN and length == 4:
+        return line_body(meson_nodes, term_nodes, weight_codes, resident_pick)
+    return wide_body(meson_nodes, term_nodes, weight_codes, resident_pick)
+
+
 def solution(mesh):
     in_specs = (P(None, ("grp", "node"), "sub", "rep"), P("grp", None), P("grp"), P("grp"))
     out_specs = P(None, ("grp", "node"), "sub", "rep")

time: 192 us -> 73.2 us (0.38)
  waiting for transfers between devices: 79.2 us -> 0 us
  Pallas kernels: 0 us -> 69.4 us
  blocking collectives: 54.3 us -> 0 us
  matrix products: 14.4 us -> 0 us
  between operations: 13.4 us -> 0.01 us
  local copies, waits for them, and re-layouts: 15.1 us -> 3.62 us
  starting transfers between devices: 10.3 us -> 0 us
  other arithmetic: 4.75 us -> 0 us
    pallas_call x0 -> x1, Pallas kernels: none -> 69.4 us  [line_body(): pl.pallas_call(functools.partial(line_kernel, length, owned, terms), out_...]
    all_to_all x2 -> x0, blocking collectives: 54.3 us -> none  [the longest x1 27.2 us: body(): lax.all_to_all(picked, 'node', split_axis=3, concat_axis=3, tiled=True)]
    all_gather x4 -> x0, waiting for transfers between devices: 43.4 us -> none  [the longest x1 20.9 us: body(): lax.all_gather(right_band, 'sub', axis=2, tiled=True)]
    all_to_all x2 -> x0, waiting for transfers between devices: 35 us -> none  [the longest x1 23.7 us: body(): lax.all_to_all(banded, 'node', split_axis=2, concat_axis=1, tiled=True)]
    dot_general x9 -> x0, matrix products: 14.4 us -> none  [the longest x2 4.7 us: complex_step(): jnp.einsum('kij,kjl->kil', full_left[0], segment[1], precision=highest, p...]
    all_to_all x2 -> x0, starting transfers between devices: 10.1 us -> none  [the longest x1 5.41 us: body(): lax.all_to_all(banded, 'node', split_axis=2, concat_axis=1, tiled=True)]
    reshape x5 -> x0, local copies, waits for them, and re-layouts: 6.76 us -> none  [the longest x2 3.53 us: body(): banded = meson_nodes.reshape(2, owned, node_count, band * col_count)]
    gather x5 -> x0, local copies, waits for them, and re-layouts: 4.2 us -> none  [the longest x1 1.67 us: body(): picked = jnp.take(spread, wanted, axis=1)]
  transfers between devices with their start and end apart: 6 -> 0, of which waited for: 5 -> 0; matrix products, arithmetic and copies ran while one was open for 5% -> 0% of each run, Pallas kernels for 0% -> 0%
where the time goes in v2:
time: 73.2 us; the launch traced here: 73 us
  Pallas kernels  69.4 us (95%)
  local copies, waits for them, and re-layouts  3.62 us (5%)
    pallas_call x1, Pallas kernels, line_body(): pl.pallas_call(functools.partial(line_kernel, length, owned, terms), out_...  69.4 us
    unnamed x2, local copies, waits for them, and re-layouts  3.62 us

profile of v2, /device:TPU:1, one launch (start us, length us, event | category | flops | bytes accessed | tf_op | source)
XLA Modules:
  0.0 73.0 jit_solution(8101056835732111402)
XLA Ops:
  0.0 1.3 %copy.5.tn_ref = s32[4,2]{1,0:T(4,128)} copy(s32[4,2]{0,1:T(2,128)} %param.5) | data formatting | bytes 64 | tf_op args[1]
  1.3 69.4 %shard_map.46 = f32[2,2,256,256]{3,2,1,0:T(8,128)} custom-call(f32[2,2,256,256]{3,2,1,0:T(8,128)} %x_ref.1, s32[4,2]{1,0:T(4,128)} %copy.5.tn_ref, s32[4]{0:T(128)} %wc_ref.1, s32[8]{0:T(128)} %rp_ref.1), custom_call_target="tpu_custom_call" | custom-call | tf_op jit(solution)/shard_map/pallas_call | solution.py:419
  70.7 2.3 %copy.7 = f32[2,2,256,256]{3,2,1,0:T(8,128)} copy(f32[2,2,256,256]{3,2,1,0:T(8,128)} %shard_map.46) | data formatting | bytes 2097152

commit v3 on v2

--- a/solution.py
+++ b/solution.py
@@ -94,7 +94,7 @@
 
 
 MESH = pl.DeviceIdType.MESH
-PIECES = 2
+PIECES = 4
 FOREIGN = 2
 
 
@@ -217,8 +217,8 @@
             local.append(copy)
         c_copy(z, j, m, r, own_at(j, m, r)).start()
 
-    firsts = [tn_ref[t, 0] for t in range(terms)]
-    seconds = [tn_ref[t, 1] for t in range(terms)]
+    firsts = [tn_ref[0, t] for t in range(terms)]
+    seconds = [tn_ref[1, t] for t in range(terms)]
     spots = (length - 2) * owned
 
     def holds(owner, n):
@@ -440,7 +440,7 @@
         compiler_params=pltpu.CompilerParams(
             collective_id=0, has_side_effects=True, vmem_limit_bytes=56 << 20
         ),
-    )(meson_nodes, term_nodes, weight_codes, resident_pick)
+    )(meson_nodes, term_nodes.T, weight_codes, resident_pick)
 
 
 def body(meson_nodes, term_nodes, weight_codes, resident_pick):

time: 73.2 us -> 71 us (0.970)
  local copies, waits for them, and re-layouts: 3.62 us -> 2.29 us
  Pallas kernels: 69.4 us -> 68.5 us
    unnamed x2 -> x1, local copies, waits for them, and re-layouts: 3.62 us -> 2.29 us
    pallas_call x1, Pallas kernels: 69.4 us -> 68.5 us  [line_body(): pl.pallas_call(functools.partial(line_kernel, length, owned, terms), out_...]
where the time goes in v3:
time: 71 us; the launch traced here: 70.8 us
  Pallas kernels  68.5 us (96%)
  local copies, waits for them, and re-layouts  2.29 us (3%)
    pallas_call x1, Pallas kernels, line_body(): pl.pallas_call(functools.partial(line_kernel, length, owned, terms), out_...  68.5 us
    unnamed x1, local copies, waits for them, and re-layouts  2.29 us

profile of v3, /device:TPU:1, one launch (start us, length us, event | category | flops | bytes accessed | tf_op | source)
XLA Modules:
  0.0 70.8 jit_solution(8281652200350137005)
XLA Ops:
  0.0 68.5 %shard_map.46 = f32[2,2,256,256]{3,2,1,0:T(8,128)} custom-call(f32[2,2,256,256]{3,2,1,0:T(8,128)} %x_ref.1, s32[2,4]{1,0:T(2,128)} %bitcast.1, s32[4]{0:T(128)} %wc_ref.1, s32[8]{0:T(128)} %rp_ref.1), custom_call_target="tpu_custom_call" | custom-call | tf_op jit(solution)/shard_map/pallas_call | solution.py:419
  68.5 2.3 %copy.6 = f32[2,2,256,256]{3,2,1,0:T(8,128)} copy(f32[2,2,256,256]{3,2,1,0:T(8,128)} %shard_map.46) | data formatting | bytes 2097152
